TPU v7x, 32 devices: a whole 2x2x4 slice. The times are simulated.
32 devices in a mesh: blocks: 2 (over y), tile: 16 (over z, x, core).
Axes of the slice: x: 2, y: 2, z: 4, core: 2. Of those that a mesh axis runs over, the one named last changes fastest.
Arguments:
- raw_views: bfloat16 [8, 1024, 32, 128], P(None, ('blocks', 'tile')), parts along dimension 1, as said below
- spread_taps: float32 [8, 2, 3, 31], replicated, may hold values from 0.0001 to 1, as said below
Outputs:
- estimate: float32 [1024, 32, 128], P(('blocks', 'tile')), parts along dimension 0
There are 2 independent parts, one for each index of `blocks`. A program takes and returns all parts, laid end to end along the dimension named above; an argument that names none is the same for every part. Nothing has to cross between parts.
Inputs may be any that keep to these rules, and one draw needn't show every extreme that they name: `raw_views`: every entry is positive. `spread_taps`: every tap is positive.
All inputs are finite; a program needn't handle non-finite values.
Results may differ from a plain program's by a relative error of at most 0.0031.
Values may be sent and summed in bfloat16 or wider, within the bound.
No kernel may reach another device: no remote copies, remote signals or barrier semaphores. Data moves between devices by JAX's collectives and lax.ppermute only.
A program may use at most 64 MiB of HBM per device.

v0:
```python
import functools

import jax
import jax.numpy as jnp
from jax import lax
from jax.experimental import pallas as pl
from jax.experimental.pallas import tpu as pltpu
from jax.sharding import PartitionSpec as P

ITERS = 2
LANES = 128
F32 = jnp.float32
BF16 = jnp.bfloat16


def toeplitz(row, rows, offset):
    lanes = row.shape[-1]
    wide = jnp.broadcast_to(row, (rows, lanes))
    return pltpu.roll(wide, (-offset) % lanes, 1, stride=1, stride_axis=0)


def depth_table(row, planes, halo, radius):
    return toeplitz(row, planes, radius - halo)


def width_table(row, width, radius):
    table = toeplitz(row, width, radius)
    r = lax.broadcasted_iota(jnp.int32, table.shape, 0)
    l = lax.broadcasted_iota(jnp.int32, table.shape, 1)
    return jnp.where(jnp.abs(l - r) <= radius, table, 0.0)


def height_table(rows, height, radius):
    lane = lax.broadcasted_iota(jnp.int32, (height, rows[0].shape[-1]), 1)
    table = jnp.zeros(lane.shape, F32)
    for t, row in enumerate(rows):
        part = toeplitz(row, height, radius - t * height)
        table = jnp.where(lane // height == t, part, table)
    return table[:, : len(rows) * height]


def store_width_table(bx_ref, rows, width, radius):
    for t, row in enumerate(rows):
        for s in range(len(rows)):
            block = (
                width_table(row, width, radius)
                if s == t
                else jnp.zeros((width, width), F32)
            )
            bx_ref[pl.ds(t * width, width), pl.ds(s * width, width)] = block.astype(BF16)


def column(parts, y):
    return jnp.concatenate([p[y] for p in parts], axis=0)


def width_pass(zs_at, bx, xs_ref, height, planes, terms, width, group):
    for g in range(height // group):
        lhs = jnp.concatenate(
            [
                jnp.concatenate([zs_at(y, t) for t in range(terms)], axis=1)
                for y in range(g * group, (g + 1) * group)
            ],
            axis=0,
        )
        out = jnp.dot(lhs, bx, preferred_element_type=F32)
        for t in range(terms):
            xs_ref[t, pl.ds(g * group * planes, group * planes), :] = out[
                :, t * width : (t + 1) * width
            ]


def height_pass(xs_ref, by, height, planes, terms, width, emit):
    for z in range(0, planes, 2):
        rhs = jnp.concatenate(
            [
                jnp.concatenate(
                    [
                        xs_ref[t, pl.ds(zz, height, stride=planes), :].astype(BF16)
                        for t in range(terms)
                    ],
                    axis=0,
                )
                for zz in (z, z + 1)
            ],
            axis=1,
        )
        out = jnp.dot(by, rhs, preferred_element_type=F32)
        emit(z, out[:, :width])
        emit(z + 1, out[:, width:])


def swap_out(qs_ref, lo_at, hi_at, height, planes):
    half = planes // 2
    for y in range(height):
        col = qs_ref[pl.ds(y, planes, stride=height), :].astype(BF16)
        lo_at(y, col[:half])
        hi_at(y, col[half:])


def first_body(scales_ref, raw_ref, est_ref, lo_ref, hi_ref):
    views, planes, height, width = raw_ref.shape
    for z in range(planes):
        acc = scales_ref[0] * raw_ref[0, z].astype(F32)
        for v in range(1, views):
            acc = acc + scales_ref[v] * raw_ref[v, z].astype(F32)
        est_ref[pl.ds(z * height, height), :] = acc / views

    def put(ref):
        def at(y, value):
            ref[y] = value
        return at

    swap_out(est_ref, put(lo_ref), put(hi_ref), height, planes)


def forward_body(radius, scales_ref, taps_ref, flip_ref, before, lo, hi, after, raw_ref,
                 qlo_ref, qhi_ref, bz_ref, bx_ref, zs_ref, xs_ref, qs_ref):
    views, planes, height, width = raw_ref.shape
    terms = taps_ref.shape[1]
    half = planes // 2
    for v in range(views):
        for t in range(terms):
            bz_ref[pl.ds((v * terms + t) * planes, planes), :] = depth_table(
                taps_ref[v, t, 0:1, :], planes, half, radius
            ).astype(BF16)[:, : 2 * planes]
    parts = (before, lo, hi, after)
    for y in range(0, height, 2):
        rhs = jnp.concatenate([column(parts, y), column(parts, y + 1)], axis=1)
        out = jnp.dot(bz_ref[...], rhs, preferred_element_type=F32).astype(BF16)
        zs_ref[y] = out[:, :width]
        zs_ref[y + 1] = out[:, width:]

    def view(v, carry):
        store_width_table(bx_ref, [flip_ref[v, t, 2:3, :] for t in range(terms)], width, radius)
        by = height_table([taps_ref[v, t, 1:2, :] for t in range(terms)], height, radius).astype(BF16)

        def zs_at(y, t):
            start = pl.multiple_of((v * terms + t) * planes, planes)
            return zs_ref[y, pl.ds(start, planes), :]

        width_pass(zs_at, bx_ref[...], xs_ref, height, planes, terms, width, 8)

        def emit(z, blurred):
            scaled = scales_ref[v] * raw_ref[v, z].astype(F32)
            qs_ref[pl.ds(z * height, height), :] = scaled / blurred

        height_pass(xs_ref, by, height, planes, terms, width, emit)

        def put(ref):
            def at(y, value):
                ref[v, y] = value
            return at

        swap_out(qs_ref, put(qlo_ref), put(qhi_ref), height, planes)
        return carry

    lax.fori_loop(0, views, view, 0)


def backward_body(radius, last, taps_ref, flip_ref, before, lo, hi, after, est_ref, *refs):
    if last:
        new_ref, bx_ref, zs_ref, xs_ref, fac_ref = refs
    else:
        new_ref, rlo_ref, rhi_ref, bx_ref, zs_ref, xs_ref, fac_ref = refs
    views, height, half, width = lo.shape
    planes = 2 * half
    terms = taps_ref.shape[1]
    fac_ref[...] = jnp.ones(fac_ref.shape, F32)

    def view(v, carry):
        bz = jnp.concatenate(
            [depth_table(flip_ref[v, t, 0:1, :], planes, half, radius) for t in range(terms)],
            axis=0,
        ).astype(BF16)[:, : 2 * planes]
        store_width_table(bx_ref, [taps_ref[v, t, 2:3, :] for t in range(terms)], width, radius)
        by = height_table([flip_ref[v, t, 1:2, :] for t in range(terms)], height, radius).astype(BF16)
        parts = [ref.at[v] for ref in (before, lo, hi, after)]
        for y in range(0, height, 2):
            rhs = jnp.concatenate([column(parts, y), column(parts, y + 1)], axis=1)
            out = jnp.dot(bz, rhs, preferred_element_type=F32).astype(BF16)
            zs_ref[y] = out[:, :width]
            zs_ref[y + 1] = out[:, width:]

        def zs_at(y, t):
            return zs_ref[y, t * planes : (t + 1) * planes, :]

        width_pass(zs_at, bx_ref[...], xs_ref, height, planes, terms, width, 8)

        def emit(z, blurred):
            rows = pl.ds(z * height, height)
            fac_ref[rows, :] = fac_ref[rows, :] * blurred

        height_pass(xs_ref, by, height, planes, terms, width, emit)
        return carry

    lax.fori_loop(0, views, view, 0)
    new_ref[...] = est_ref[...] * fac_ref[...]
    if not last:
        def put(ref):
            def at(y, value):
                ref[y] = value
            return at

        swap_out(new_ref, put(rlo_ref), put(rhi_ref), height, planes)


VMEM_SPEC = pl.BlockSpec(memory_space=pltpu.VMEM)
SMEM_SPEC = pl.BlockSpec(memory_space=pltpu.SMEM)


def local(raw_views, spread_taps):
    views, planes, height, width = raw_views.shape
    terms, tap_count = spread_taps.shape[1], spread_taps.shape[3]
    radius = (tap_count - 1) // 2
    half = planes // 2
    cells = planes * height
    size = lax.axis_size("tile")
    taps = spread_taps.astype(BF16).astype(F32)
    lane_pad = ((0, 0), (0, 0), (0, 0), (0, LANES - tap_count))
    flip = jnp.pad(taps[:, :, :, ::-1], lane_pad)
    taps = jnp.pad(taps, lane_pad)

    totals = lax.psum(jnp.sum(raw_views, axis=(1, 2, 3), dtype=F32), "tile")
    scales = jnp.mean(totals) / totals

    up = [(i, i + 1) for i in range(size - 1)]
    down = [(i + 1, i) for i in range(size - 1)]
    flat = jax.ShapeDtypeStruct((cells, width), F32)
    slab = jax.ShapeDtypeStruct((height, half, width), BF16)
    slabs = jax.ShapeDtypeStruct((views, height, half, width), BF16)
    params = pltpu.CompilerParams(vmem_limit_bytes=48 * 1024 * 1024)

    estimate, lo, hi = pl.pallas_call(
        first_body,
        out_shape=(flat, slab, slab),
        in_specs=[SMEM_SPEC, VMEM_SPEC],
        out_specs=(VMEM_SPEC,) * 3,
        compiler_params=params,
        name="first",
    )(scales, raw_views)

    forward = pl.pallas_call(
        functools.partial(forward_body, radius),
        out_shape=(slabs, slabs),
        in_specs=[SMEM_SPEC] + [VMEM_SPEC] * 7,
        out_specs=(VMEM_SPEC,) * 2,
        scratch_shapes=[
            pltpu.VMEM((views * terms * planes, 2 * planes), BF16),
            pltpu.VMEM((terms * width, terms * width), BF16),
            pltpu.VMEM((height, views * terms * planes, width), BF16),
            pltpu.VMEM((terms, cells, width), F32),
            pltpu.VMEM((cells, width), F32),
        ],
        compiler_params=params,
        name="forward",
    )

    def backward(last):
        return pl.pallas_call(
            functools.partial(backward_body, radius, last),
            out_shape=(flat,) if last else (flat, slab, slab),
            in_specs=[VMEM_SPEC] * 7,
            out_specs=(VMEM_SPEC,) * (1 if last else 3),
            scratch_shapes=[
                pltpu.VMEM((terms * width, terms * width), BF16),
                pltpu.VMEM((height, terms * planes, width), BF16),
                pltpu.VMEM((terms, cells, width), F32),
                pltpu.VMEM((cells, width), F32),
            ],
            compiler_params=params,
            name="backward",
        )

    for iteration in range(ITERS):
        last = iteration == ITERS - 1
        before = lax.ppermute(hi, "tile", up)
        after = lax.ppermute(lo, "tile", down)
        qlo, qhi = forward(scales, taps, flip, before, lo, hi, after, raw_views)
        qbefore = lax.ppermute(qhi, "tile", up)
        qafter = lax.ppermute(qlo, "tile", down)
        out = backward(last)(taps, flip, qbefore, qlo, qhi, qafter, estimate)
        if last:
            (estimate,) = out
        else:
            estimate, lo, hi = out
    return estimate.reshape(planes, height, width)


def solution(mesh):
    return jax.shard_map(
        local,
        mesh=mesh,
        in_specs=(P(None, ("blocks", "tile"), None, None), P()),
        out_specs=P(("blocks", "tile"), None, None),
        check_vma=False,
    )
```

profile of v0, /device:TPU:1, one launch (start us, length us, event | category | flops | bytes accessed | tf_op | source)
XLA Modules:
  0.0 150.4 jit_solution(11622515020800558098)
XLA Ops:
  0.0 0.0 copy-start
  0.0 0.0 copy-start.1
  0.0 2.2 %convert_reduce_fusion = f32[8]{0:T(128)S(1)} fusion(bf16[8,32,32,128]{3,2,1,0:T(8,128)(2,1)} %raw_ref.5), kind=kLoop, calls=%fused_computation | loop fusion | flops 2097144 | bytes 2097184 | tf_op jit(solution)/shard_map/reduce_sum | solution.py:224
  2.2 30.5 %psum.7 = f32[8]{0:T(128)S(1)} all-reduce(f32[8]{0:T(128)S(1)} %convert_reduce_fusion), channel_id=1, replica_groups=mesh['blocks'=2,'tile'=16] {'tile'}, use_global_device_ids=true, to_apply=%region_1.2 | all-reduce | flops 8 | bytes 64 | tf_op jit(solution)/shard_map/psum | solution.py:224
  32.7 0.6 reduce_sum.19
  34.0 0.0 copy-done
  34.0 1.2 first.1
  35.3 3.0 %collective-permute-start = (bf16[32,16,128]{2,1,0:T(8,128)(2,1)S(1)}, bf16[32,16,128]{2,1,0:T(8,128)(2,1)S(1)}, u32[]{:S(2)}, u32[]{:S(2)}) collective-permute-start(bf16[32,16,128]{2,1,0:T(8,128)(2,1)S(1)} %get-tuple-element.15.hi), channel_id=1, source_target_pairs={{0,1},{1,2},{2,3},{3,4},{4,5},{5,6},{6,7},{7,8},{8,9},{9,10},{10,1... | collective-permute-start | bytes 393224 | tf_op jit(solution)/shard_map/ppermute | solution.py:277
  38.2 4.6 %collective-permute-start.1 = (bf16[32,16,128]{2,1,0:T(8,128)(2,1)S(1)}, bf16[32,16,128]{2,1,0:T(8,128)(2,1)S(1)}, u32[]{:S(2)}, u32[]{:S(2)}) collective-permute-start(bf16[32,16,128]{2,1,0:T(8,128)(2,1)S(1)} %get-tuple-element.16.lo), channel_id=1, source_target_pairs={{1,0},{2,1},{3,2},{4,3},{5,4},{6,5},{7,6},{8,7},{9,8},{10,9},{11,1... | collective-permute-start | bytes 393224 | tf_op jit(solution)/shard_map/ppermute | solution.py:278
  42.9 0.0 copy-done.1
  42.9 0.1 rev.3
  43.0 0.0 collective-permute-done.before
  43.1 1.5 collective-permute-done.1.after
  44.5 12.3 %forward.2 = (bf16[8,32,16,128]{3,2,1,0:T(8,128)(2,1)S(1)}, bf16[8,32,16,128]{3,2,1,0:T(8,128)(2,1)S(1)}) custom-call(f32[8]{0:T(128)S(1)} %broadcast_divide_fusion.scales_ref, f32[8,2,3,128]{3,2,1,0:T(4,128)S(1)} %pad.7.taps_ref, f32[8,2,3,128]{3,2,1,0:T(4,128)S(1)} %pad.8.flip_ref, bf16[32,16,128]{2,1,0:T(8,128)(2,1)S(1)} %collective-permute-done.before, ...), custom_call_target="tpu_custom_call" | custom-call | tf_op jit(solution)/shard_map/forward/pallas_call | solution.py:279
  56.8 1.9 %collective-permute-start.2 = (bf16[8,32,16,128]{3,2,1,0:T(8,128)(2,1)S(1)}, bf16[8,32,16,128]{3,2,1,0:T(8,128)(2,1)S(1)}, u32[]{:S(2)}, u32[]{:S(2)}) collective-permute-start(bf16[8,32,16,128]{3,2,1,0:T(8,128)(2,1)S(1)} %get-tuple-element.17.hi), channel_id=1, source_target_pairs={{0,1},{1,2},{2,3},{3,4},{4,5},{5,6},{6,7},{7,8},{8,9},{9,10},{10,1... | collective-permute-start | bytes 3145736 | tf_op jit(solution)/shard_map/ppermute | solution.py:280
  58.8 2.5 %collective-permute-start.3 = (bf16[8,32,16,128]{3,2,1,0:T(8,128)(2,1)S(1)}, bf16[8,32,16,128]{3,2,1,0:T(8,128)(2,1)S(1)}, u32[]{:S(2)}, u32[]{:S(2)}) collective-permute-start(bf16[8,32,16,128]{3,2,1,0:T(8,128)(2,1)S(1)} %get-tuple-element.18.lo), channel_id=1, source_target_pairs={{1,0},{2,1},{3,2},{4,3},{5,4},{6,5},{7,6},{8,7},{9,8},{10,9},{11,1... | collective-permute-start | bytes 3145736 | tf_op jit(solution)/shard_map/ppermute | solution.py:281
  61.2 20.5 %collective-permute-done.2.before = bf16[8,32,16,128]{3,2,1,0:T(8,128)(2,1)S(1)} collective-permute-done((bf16[8,32,16,128]{3,2,1,0:T(8,128)(2,1)S(1)}, bf16[8,32,16,128]{3,2,1,0:T(8,128)(2,1)S(1)}, u32[]{:S(2)}, u32[]{:S(2)}) %collective-permute-start.2) | collective-permute-done | bytes 1048608 | tf_op jit(solution)/shard_map/ppermute | solution.py:280
  81.7 0.0 collective-permute-done.3.after
  81.7 10.1 %backward.2 = (f32[1024,128]{1,0:T(8,128)S(1)}, bf16[32,16,128]{2,1,0:T(8,128)(2,1)S(1)}, bf16[32,16,128]{2,1,0:T(8,128)(2,1)S(1)}) custom-call(f32[8,2,3,128]{3,2,1,0:T(4,128)S(1)} %pad.7.taps_ref, f32[8,2,3,128]{3,2,1,0:T(4,128)S(1)} %pad.8.flip_ref, bf16[8,32,16,128]{3,2,1,0:T(8,128)(2,1)S(1)} %collective-permute-done.2.before, ...), custom_call_target="tpu_custom_call" | custom-call | tf_op jit(solution)/shard_map/backward/pallas_call | solution.py:282
  91.8 4.4 %collective-permute-start.4 = (bf16[32,16,128]{2,1,0:T(8,128)(2,1)S(1)}, bf16[32,16,128]{2,1,0:T(8,128)(2,1)S(1)}, u32[]{:S(2)}, u32[]{:S(2)}) collective-permute-start(bf16[32,16,128]{2,1,0:T(8,128)(2,1)S(1)} %get-tuple-element.20.hi), channel_id=1, source_target_pairs={{0,1},{1,2},{2,3},{3,4},{4,5},{5,6},{6,7},{7,8},{8,9},{9,10},{10,1... | collective-permute-start | bytes 393224 | tf_op jit(solution)/shard_map/ppermute | solution.py:277
  96.3 1.9 %collective-permute-start.5 = (bf16[32,16,128]{2,1,0:T(8,128)(2,1)S(1)}, bf16[32,16,128]{2,1,0:T(8,128)(2,1)S(1)}, u32[]{:S(2)}, u32[]{:S(2)}) collective-permute-start(bf16[32,16,128]{2,1,0:T(8,128)(2,1)S(1)} %get-tuple-element.21.lo), channel_id=1, source_target_pairs={{1,0},{2,1},{3,2},{4,3},{5,4},{6,5},{7,6},{8,7},{9,8},{10,9},{11,1... | collective-permute-start | bytes 393224 | tf_op jit(solution)/shard_map/ppermute | solution.py:278
  98.2 1.4 collective-permute-done.4.before
  99.5 3.0 %collective-permute-done.5.after = bf16[32,16,128]{2,1,0:T(8,128)(2,1)S(1)} collective-permute-done((bf16[32,16,128]{2,1,0:T(8,128)(2,1)S(1)}, bf16[32,16,128]{2,1,0:T(8,128)(2,1)S(1)}, u32[]{:S(2)}, u32[]{:S(2)}) %collective-permute-start.5) | collective-permute-done | bytes 131104 | tf_op jit(solution)/shard_map/ppermute | solution.py:278
  102.5 12.3 %forward.3 = (bf16[8,32,16,128]{3,2,1,0:T(8,128)(2,1)S(1)}, bf16[8,32,16,128]{3,2,1,0:T(8,128)(2,1)S(1)}) custom-call(f32[8]{0:T(128)S(1)} %broadcast_divide_fusion.scales_ref, f32[8,2,3,128]{3,2,1,0:T(4,128)S(1)} %pad.7.taps_ref, f32[8,2,3,128]{3,2,1,0:T(4,128)S(1)} %pad.8.flip_ref, bf16[32,16,128]{2,1,0:T(8,128)(2,1)S(1)} %collective-permute-done.4.before, ...), custom_call_target="tpu_custom_call" | custom-call | tf_op jit(solution)/shard_map/forward/pallas_call | solution.py:279
  114.8 1.9 %collective-permute-start.6 = (bf16[8,32,16,128]{3,2,1,0:T(8,128)(2,1)S(1)}, bf16[8,32,16,128]{3,2,1,0:T(8,128)(2,1)S(1)}, u32[]{:S(2)}, u32[]{:S(2)}) collective-permute-start(bf16[8,32,16,128]{3,2,1,0:T(8,128)(2,1)S(1)} %get-tuple-element.22.hi), channel_id=1, source_target_pairs={{0,1},{1,2},{2,3},{3,4},{4,5},{5,6},{6,7},{7,8},{8,9},{9,10},{10,1... | collective-permute-start | bytes 3145736 | tf_op jit(solution)/shard_map/ppermute | solution.py:280
  116.8 2.5 %collective-permute-start.7 = (bf16[8,32,16,128]{3,2,1,0:T(8,128)(2,1)S(1)}, bf16[8,32,16,128]{3,2,1,0:T(8,128)(2,1)S(1)}, u32[]{:S(2)}, u32[]{:S(2)}) collective-permute-start(bf16[8,32,16,128]{3,2,1,0:T(8,128)(2,1)S(1)} %get-tuple-element.23.lo), channel_id=1, source_target_pairs={{1,0},{2,1},{3,2},{4,3},{5,4},{6,5},{7,6},{8,7},{9,8},{10,9},{11,1... | collective-permute-start | bytes 3145736 | tf_op jit(solution)/shard_map/ppermute | solution.py:281
  119.2 20.5 %collective-permute-done.6.before = bf16[8,32,16,128]{3,2,1,0:T(8,128)(2,1)S(1)} collective-permute-done((bf16[8,32,16,128]{3,2,1,0:T(8,128)(2,1)S(1)}, bf16[8,32,16,128]{3,2,1,0:T(8,128)(2,1)S(1)}, u32[]{:S(2)}, u32[]{:S(2)}) %collective-permute-start.6) | collective-permute-done | bytes 1048608 | tf_op jit(solution)/shard_map/ppermute | solution.py:280
  139.7 0.0 collective-permute-done.7.after
  139.7 10.6 %backward.3 = f32[1024,128]{1,0:T(8,128)} custom-call(f32[8,2,3,128]{3,2,1,0:T(4,128)S(1)} %pad.7.taps_ref, f32[8,2,3,128]{3,2,1,0:T(4,128)S(1)} %pad.8.flip_ref, bf16[8,32,16,128]{3,2,1,0:T(8,128)(2,1)S(1)} %collective-permute-done.6.before, bf16[8,32,16,128]{3,2,1,0:T(8,128)(2,1)S(1)} %get-tuple-element.23.lo, ...), custom_call_target="tpu_custom_call" | custom-call | tf_op jit(solution)/shard_map/backward/pallas_call | solution.py:282
  (4 shorter events, 0.0 us)
Async XLA Ops:
  0.0 34.0 %copy-start = (bf16[8,32,32,128]{3,2,1,0:T(8,128)(2,1)S(1)}, bf16[8,32,32,128]{3,2,1,0:T(8,128)(2,1)}, u32[]{:S(2)}) copy-start(bf16[8,32,32,128]{3,2,1,0:T(8,128)(2,1)} %raw_ref.5) | copy-start | bytes 6291460
  0.0 42.9 %copy-start.1 = (f32[8,2,3,31]{3,1,2,0:T(2,128)S(1)}, f32[8,2,3,31]{3,1,2,0:T(2,128)}, u32[]{:S(2)}) copy-start(f32[8,2,3,31]{3,1,2,0:T(2,128)} %param.3) | copy-start | bytes 17860
  35.3 7.8 %collective-permute-start = (bf16[32,16,128]{2,1,0:T(8,128)(2,1)S(1)}, bf16[32,16,128]{2,1,0:T(8,128)(2,1)S(1)}, u32[]{:S(2)}, u32[]{:S(2)}) collective-permute-start(bf16[32,16,128]{2,1,0:T(8,128)(2,1)S(1)} %get-tuple-element.15.hi), channel_id=1, source_target_pairs={{0,1},{1,2},{2,3},{3,4},{4,5},{5,6},{6,7},{7,8},{8,9},{9,10},{10,1... | collective-permute-start | bytes 393224 | tf_op jit(solution)/shard_map/ppermute | solution.py:277
  38.2 6.3 %collective-permute-start.1 = (bf16[32,16,128]{2,1,0:T(8,128)(2,1)S(1)}, bf16[32,16,128]{2,1,0:T(8,128)(2,1)S(1)}, u32[]{:S(2)}, u32[]{:S(2)}) collective-permute-start(bf16[32,16,128]{2,1,0:T(8,128)(2,1)S(1)} %get-tuple-element.16.lo), channel_id=1, source_target_pairs={{1,0},{2,1},{3,2},{4,3},{5,4},{6,5},{7,6},{8,7},{9,8},{10,9},{11,1... | collective-permute-start | bytes 393224 | tf_op jit(solution)/shard_map/ppermute | solution.py:278
  56.8 24.9 %collective-permute-start.2 = (bf16[8,32,16,128]{3,2,1,0:T(8,128)(2,1)S(1)}, bf16[8,32,16,128]{3,2,1,0:T(8,128)(2,1)S(1)}, u32[]{:S(2)}, u32[]{:S(2)}) collective-permute-start(bf16[8,32,16,128]{3,2,1,0:T(8,128)(2,1)S(1)} %get-tuple-element.17.hi), channel_id=1, source_target_pairs={{0,1},{1,2},{2,3},{3,4},{4,5},{5,6},{6,7},{7,8},{8,9},{9,10},{10,1... | collective-permute-start | bytes 3145736 | tf_op jit(solution)/shard_map/ppermute | solution.py:280
  58.8 23.0 %collective-permute-start.3 = (bf16[8,32,16,128]{3,2,1,0:T(8,128)(2,1)S(1)}, bf16[8,32,16,128]{3,2,1,0:T(8,128)(2,1)S(1)}, u32[]{:S(2)}, u32[]{:S(2)}) collective-permute-start(bf16[8,32,16,128]{3,2,1,0:T(8,128)(2,1)S(1)} %get-tuple-element.18.lo), channel_id=1, source_target_pairs={{1,0},{2,1},{3,2},{4,3},{5,4},{6,5},{7,6},{8,7},{9,8},{10,9},{11,1... | collective-permute-start | bytes 3145736 | tf_op jit(solution)/shard_map/ppermute | solution.py:281
  91.8 7.7 %collective-permute-start.4 = (bf16[32,16,128]{2,1,0:T(8,128)(2,1)S(1)}, bf16[32,16,128]{2,1,0:T(8,128)(2,1)S(1)}, u32[]{:S(2)}, u32[]{:S(2)}) collective-permute-start(bf16[32,16,128]{2,1,0:T(8,128)(2,1)S(1)} %get-tuple-element.20.hi), channel_id=1, source_target_pairs={{0,1},{1,2},{2,3},{3,4},{4,5},{5,6},{6,7},{7,8},{8,9},{9,10},{10,1... | collective-permute-start | bytes 393224 | tf_op jit(solution)/shard_map/ppermute | solution.py:277
  96.3 6.3 %collective-permute-start.5 = (bf16[32,16,128]{2,1,0:T(8,128)(2,1)S(1)}, bf16[32,16,128]{2,1,0:T(8,128)(2,1)S(1)}, u32[]{:S(2)}, u32[]{:S(2)}) collective-permute-start(bf16[32,16,128]{2,1,0:T(8,128)(2,1)S(1)} %get-tuple-element.21.lo), channel_id=1, source_target_pairs={{1,0},{2,1},{3,2},{4,3},{5,4},{6,5},{7,6},{8,7},{9,8},{10,9},{11,1... | collective-permute-start | bytes 393224 | tf_op jit(solution)/shard_map/ppermute | solution.py:278
  114.8 24.9 %collective-permute-start.6 = (bf16[8,32,16,128]{3,2,1,0:T(8,128)(2,1)S(1)}, bf16[8,32,16,128]{3,2,1,0:T(8,128)(2,1)S(1)}, u32[]{:S(2)}, u32[]{:S(2)}) collective-permute-start(bf16[8,32,16,128]{3,2,1,0:T(8,128)(2,1)S(1)} %get-tuple-element.22.hi), channel_id=1, source_target_pairs={{0,1},{1,2},{2,3},{3,4},{4,5},{5,6},{6,7},{7,8},{8,9},{9,10},{10,1... | collective-permute-start | bytes 3145736 | tf_op jit(solution)/shard_map/ppermute | solution.py:280
  116.8 23.0 %collective-permute-start.7 = (bf16[8,32,16,128]{3,2,1,0:T(8,128)(2,1)S(1)}, bf16[8,32,16,128]{3,2,1,0:T(8,128)(2,1)S(1)}, u32[]{:S(2)}, u32[]{:S(2)}) collective-permute-start(bf16[8,32,16,128]{3,2,1,0:T(8,128)(2,1)S(1)} %get-tuple-element.23.lo), channel_id=1, source_target_pairs={{1,0},{2,1},{3,2},{4,3},{5,4},{6,5},{7,6},{8,7},{9,8},{10,9},{11,1... | collective-permute-start | bytes 3145736 | tf_op jit(solution)/shard_map/ppermute | solution.py:281
where the time goes:
time: 151 us; the launch traced here: 150 us
  waiting for transfers between devices  46.8 us (31%)
  Pallas kernels  46.6 us (31%)
  blocking collectives  30.5 us (20%)
  starting transfers between devices  22.7 us (15%)
  other arithmetic  2.82 us (2%)
    ppermute x2, waiting for transfers between devices, local(): qbefore = lax.ppermute(qhi, 'tile', up)  41 us
    psum x1, blocking collectives, local(): totals = lax.psum(jnp.sum(raw_views, axis=(1, 2, 3), dtype=F32), 'tile')  30.5 us
    pallas_call x2, Pallas kernels, local(): qlo, qhi = forward(scales, taps, flip, before, lo, hi, after, raw_views)  24.6 us
    pallas_call x2, Pallas kernels, local(): out = backward(last)(taps, flip, qbefore, qlo, qhi, qafter, estimate)  20.7 us
    ppermute x2, starting transfers between devices, local(): before = lax.ppermute(hi, 'tile', up)  7.38 us
    ppermute x2, starting transfers between devices, local(): after = lax.ppermute(lo, 'tile', down)  6.55 us
    ppermute x2, starting transfers between devices, local(): qafter = lax.ppermute(qlo, 'tile', down)  4.94 us
    ppermute x2, waiting for transfers between devices, local(): after = lax.ppermute(lo, 'tile', down)  4.46 us
  transfers between devices with their start and end apart: 8, of which 5 were waited for; matrix products, arithmetic and copies ran while one was open for 0% of the time, Pallas kernels for 0%

commit v1 on v0

--- a/solution.py
+++ b/solution.py
@@ -65,9 +65,10 @@
         )
         out = jnp.dot(lhs, bx, preferred_element_type=F32)
         for t in range(terms):
-            xs_ref[t, pl.ds(g * group * planes, group * planes), :] = out[
-                :, t * width : (t + 1) * width
-            ]
+            for i in range(group):
+                xs_ref[t, pl.ds((g * group + i) * (planes + 1), planes), :] = out[
+                    i * planes : (i + 1) * planes, t * width : (t + 1) * width
+                ]
 
 
 def height_pass(xs_ref, by, height, planes, terms, width, emit):
@@ -76,7 +77,7 @@
             [
                 jnp.concatenate(
                     [
-                        xs_ref[t, pl.ds(zz, height, stride=planes), :].astype(BF16)
+                        xs_ref[t, pl.ds(zz, height, stride=planes + 1), :].astype(BF16)
                         for t in range(terms)
                     ],
                     axis=0,
@@ -93,25 +94,27 @@
 def swap_out(qs_ref, lo_at, hi_at, height, planes):
     half = planes // 2
     for y in range(height):
-        col = qs_ref[pl.ds(y, planes, stride=height), :].astype(BF16)
+        col = qs_ref[pl.ds(y, planes, stride=height + 1), :].astype(BF16)
         lo_at(y, col[:half])
         hi_at(y, col[half:])
 
 
-def first_body(scales_ref, raw_ref, est_ref, lo_ref, hi_ref):
+def first_body(scales_ref, raw_ref, est_ref, lo_ref, hi_ref, qs_ref):
     views, planes, height, width = raw_ref.shape
     for z in range(planes):
         acc = scales_ref[0] * raw_ref[0, z].astype(F32)
         for v in range(1, views):
             acc = acc + scales_ref[v] * raw_ref[v, z].astype(F32)
-        est_ref[pl.ds(z * height, height), :] = acc / views
+        acc = acc / views
+        est_ref[pl.ds(z * height, height), :] = acc
+        qs_ref[pl.ds(z * (height + 1), height), :] = acc
 
     def put(ref):
         def at(y, value):
             ref[y] = value
         return at
 
-    swap_out(est_ref, put(lo_ref), put(hi_ref), height, planes)
+    swap_out(qs_ref, put(lo_ref), put(hi_ref), height, planes)
 
 
 def forward_body(radius, scales_ref, taps_ref, flip_ref, before, lo, hi, after, raw_ref,
@@ -143,7 +146,7 @@
 
         def emit(z, blurred):
             scaled = scales_ref[v] * raw_ref[v, z].astype(F32)
-            qs_ref[pl.ds(z * height, height), :] = scaled / blurred
+            qs_ref[pl.ds(z * (height + 1), height), :] = scaled / blurred
 
         height_pass(xs_ref, by, height, planes, terms, width, emit)
 
@@ -160,9 +163,9 @@
 
 def backward_body(radius, last, taps_ref, flip_ref, before, lo, hi, after, est_ref, *refs):
     if last:
-        new_ref, bx_ref, zs_ref, xs_ref, fac_ref = refs
+        new_ref, bx_ref, zs_ref, xs_ref, fac_ref, qs_ref = refs
     else:
-        new_ref, rlo_ref, rhi_ref, bx_ref, zs_ref, xs_ref, fac_ref = refs
+        new_ref, rlo_ref, rhi_ref, bx_ref, zs_ref, xs_ref, fac_ref, qs_ref = refs
     views, height, half, width = lo.shape
     planes = 2 * half
     terms = taps_ref.shape[1]
@@ -195,14 +198,19 @@
         return carry
 
     lax.fori_loop(0, views, view, 0)
-    new_ref[...] = est_ref[...] * fac_ref[...]
+    for z in range(planes):
+        rows = pl.ds(z * height, height)
+        new = est_ref[rows, :] * fac_ref[rows, :]
+        new_ref[rows, :] = new
+        if not last:
+            qs_ref[pl.ds(z * (height + 1), height), :] = new
     if not last:
         def put(ref):
             def at(y, value):
                 ref[y] = value
             return at
 
-        swap_out(new_ref, put(rlo_ref), put(rhi_ref), height, planes)
+        swap_out(qs_ref, put(rlo_ref), put(rhi_ref), height, planes)
 
 
 VMEM_SPEC = pl.BlockSpec(memory_space=pltpu.VMEM)
@@ -236,6 +244,7 @@
         out_shape=(flat, slab, slab),
         in_specs=[SMEM_SPEC, VMEM_SPEC],
         out_specs=(VMEM_SPEC,) * 3,
+        scratch_shapes=[pltpu.VMEM((planes * (height + 1), width), F32)],
         compiler_params=params,
         name="first",
     )(scales, raw_views)
@@ -249,8 +258,8 @@
             pltpu.VMEM((views * terms * planes, 2 * planes), BF16),
             pltpu.VMEM((terms * width, terms * width), BF16),
             pltpu.VMEM((height, views * terms * planes, width), BF16),
-            pltpu.VMEM((terms, cells, width), F32),
-            pltpu.VMEM((cells, width), F32),
+            pltpu.VMEM((terms, height * (planes + 1), width), F32),
+            pltpu.VMEM((planes * (height + 1), width), F32),
         ],
         compiler_params=params,
         name="forward",
@@ -265,8 +274,9 @@
             scratch_shapes=[
                 pltpu.VMEM((terms * width, terms * width), BF16),
                 pltpu.VMEM((height, terms * planes, width), BF16),
-                pltpu.VMEM((terms, cells, width), F32),
+                pltpu.VMEM((terms, height * (planes + 1), width), F32),
                 pltpu.VMEM((cells, width), F32),
+                pltpu.VMEM((planes * (height + 1), width), F32),
             ],
             compiler_params=params,
             name="backward",

time: 151 us -> 132 us (0.87)
  Pallas kernels: 46.6 us -> 27.8 us
    pallas_call x2, Pallas kernels: 24.6 us -> 13.8 us  [local(): qlo, qhi = forward(scales, taps, flip, before, lo, hi, after, raw_views)]
    pallas_call x2, Pallas kernels: 20.7 us -> 13 us  [local(): out = backward(last)(taps, flip, qbefore, qlo, qhi, qafter, estimate)]
where the time goes in v1:
time: 132 us
  waiting for transfers between devices  46.8 us (35%)
  blocking collectives  30.5 us (23%)
  Pallas kernels  27.8 us (21%)
  starting transfers between devices  22.7 us (17%)
  other arithmetic  2.82 us (2%)
    ppermute x2, waiting for transfers between devices, local(): qbefore = lax.ppermute(qhi, 'tile', up)  41 us
    psum x1, blocking collectives, local(): totals = lax.psum(jnp.sum(raw_views, axis=(1, 2, 3), dtype=F32), 'tile')  30.5 us
    pallas_call x2, Pallas kernels, local(): qlo, qhi = forward(scales, taps, flip, before, lo, hi, after, raw_views)  13.8 us
    pallas_call x2, Pallas kernels, local(): out = backward(last)(taps, flip, qbefore, qlo, qhi, qafter, estimate)  13 us
    ppermute x2, starting transfers between devices, local(): before = lax.ppermute(hi, 'tile', up)  7.36 us
    ppermute x2, starting transfers between devices, local(): after = lax.ppermute(lo, 'tile', down)  6.55 us
    ppermute x2, starting transfers between devices, local(): qafter = lax.ppermute(qlo, 'tile', down)  4.94 us
    ppermute x2, waiting for transfers between devices, local(): after = lax.ppermute(lo, 'tile', down)  4.46 us
  transfers between devices with their start and end apart: 8, of which 5 were waited for; matrix products, arithmetic and copies ran while one was open for 0% of the time, Pallas kernels for 0%

profile of v1, /device:TPU:1, one launch (start us, length us, event | category | flops | bytes accessed | tf_op | source)
XLA Modules:
  0.0 131.6 jit_solution(17795043747196066622)
XLA Ops:
  0.0 0.0 copy-start
  0.0 0.0 copy-start.1
  0.0 2.2 %convert_reduce_fusion = f32[8]{0:T(128)S(1)} fusion(bf16[8,32,32,128]{3,2,1,0:T(8,128)(2,1)} %raw_ref.5), kind=kLoop, calls=%fused_computation | loop fusion | flops 2097144 | bytes 2097184 | tf_op jit(solution)/shard_map/reduce_sum | solution.py:232
  2.2 30.5 %psum.7 = f32[8]{0:T(128)S(1)} all-reduce(f32[8]{0:T(128)S(1)} %convert_reduce_fusion), channel_id=1, replica_groups=mesh['blocks'=2,'tile'=16] {'tile'}, use_global_device_ids=true, to_apply=%region_1.2 | all-reduce | flops 8 | bytes 64 | tf_op jit(solution)/shard_map/psum | solution.py:232
  32.7 0.6 reduce_sum.19
  34.0 0.0 copy-done
  34.0 1.0 first.1
  35.0 3.0 %collective-permute-start = (bf16[32,16,128]{2,1,0:T(8,128)(2,1)S(1)}, bf16[32,16,128]{2,1,0:T(8,128)(2,1)S(1)}, u32[]{:S(2)}, u32[]{:S(2)}) collective-permute-start(bf16[32,16,128]{2,1,0:T(8,128)(2,1)S(1)} %get-tuple-element.15.hi), channel_id=1, source_target_pairs={{0,1},{1,2},{2,3},{3,4},{4,5},{5,6},{6,7},{7,8},{8,9},{9,10},{10,1... | collective-permute-start | bytes 393224 | tf_op jit(solution)/shard_map/ppermute | solution.py:287
  38.0 4.6 %collective-permute-start.1 = (bf16[32,16,128]{2,1,0:T(8,128)(2,1)S(1)}, bf16[32,16,128]{2,1,0:T(8,128)(2,1)S(1)}, u32[]{:S(2)}, u32[]{:S(2)}) collective-permute-start(bf16[32,16,128]{2,1,0:T(8,128)(2,1)S(1)} %get-tuple-element.16.lo), channel_id=1, source_target_pairs={{1,0},{2,1},{3,2},{4,3},{5,4},{6,5},{7,6},{8,7},{9,8},{10,9},{11,1... | collective-permute-start | bytes 393224 | tf_op jit(solution)/shard_map/ppermute | solution.py:288
  42.6 0.0 copy-done.1
  42.7 0.1 rev.3
  42.8 0.0 collective-permute-done.before
  42.8 1.5 %collective-permute-done.1.after = bf16[32,16,128]{2,1,0:T(8,128)(2,1)S(1)} collective-permute-done((bf16[32,16,128]{2,1,0:T(8,128)(2,1)S(1)}, bf16[32,16,128]{2,1,0:T(8,128)(2,1)S(1)}, u32[]{:S(2)}, u32[]{:S(2)}) %collective-permute-start.1) | collective-permute-done | bytes 131104 | tf_op jit(solution)/shard_map/ppermute | solution.py:288
  44.3 6.9 %forward.2 = (bf16[8,32,16,128]{3,2,1,0:T(8,128)(2,1)S(1)}, bf16[8,32,16,128]{3,2,1,0:T(8,128)(2,1)S(1)}) custom-call(f32[8]{0:T(128)S(1)} %broadcast_divide_fusion.scales_ref, f32[8,2,3,128]{3,2,1,0:T(4,128)S(1)} %pad.7.taps_ref, f32[8,2,3,128]{3,2,1,0:T(4,128)S(1)} %pad.8.flip_ref, bf16[32,16,128]{2,1,0:T(8,128)(2,1)S(1)} %collective-permute-done.before, ...), custom_call_target="tpu_custom_call" | custom-call | tf_op jit(solution)/shard_map/forward/pallas_call | solution.py:289
  51.2 1.9 %collective-permute-start.2 = (bf16[8,32,16,128]{3,2,1,0:T(8,128)(2,1)S(1)}, bf16[8,32,16,128]{3,2,1,0:T(8,128)(2,1)S(1)}, u32[]{:S(2)}, u32[]{:S(2)}) collective-permute-start(bf16[8,32,16,128]{3,2,1,0:T(8,128)(2,1)S(1)} %get-tuple-element.17.hi), channel_id=1, source_target_pairs={{0,1},{1,2},{2,3},{3,4},{4,5},{5,6},{6,7},{7,8},{8,9},{9,10},{10,1... | collective-permute-start | bytes 3145736 | tf_op jit(solution)/shard_map/ppermute | solution.py:290
  53.1 2.5 %collective-permute-start.3 = (bf16[8,32,16,128]{3,2,1,0:T(8,128)(2,1)S(1)}, bf16[8,32,16,128]{3,2,1,0:T(8,128)(2,1)S(1)}, u32[]{:S(2)}, u32[]{:S(2)}) collective-permute-start(bf16[8,32,16,128]{3,2,1,0:T(8,128)(2,1)S(1)} %get-tuple-element.18.lo), channel_id=1, source_target_pairs={{1,0},{2,1},{3,2},{4,3},{5,4},{6,5},{7,6},{8,7},{9,8},{10,9},{11,1... | collective-permute-start | bytes 3145736 | tf_op jit(solution)/shard_map/ppermute | solution.py:291
  55.6 20.5 %collective-permute-done.2.before = bf16[8,32,16,128]{3,2,1,0:T(8,128)(2,1)S(1)} collective-permute-done((bf16[8,32,16,128]{3,2,1,0:T(8,128)(2,1)S(1)}, bf16[8,32,16,128]{3,2,1,0:T(8,128)(2,1)S(1)}, u32[]{:S(2)}, u32[]{:S(2)}) %collective-permute-start.2) | collective-permute-done | bytes 1048608 | tf_op jit(solution)/shard_map/ppermute | solution.py:290
  76.1 0.0 collective-permute-done.3.after
  76.1 6.1 %backward.2 = (f32[1024,128]{1,0:T(8,128)S(1)}, bf16[32,16,128]{2,1,0:T(8,128)(2,1)S(1)}, bf16[32,16,128]{2,1,0:T(8,128)(2,1)S(1)}) custom-call(f32[8,2,3,128]{3,2,1,0:T(4,128)S(1)} %pad.7.taps_ref, f32[8,2,3,128]{3,2,1,0:T(4,128)S(1)} %pad.8.flip_ref, bf16[8,32,16,128]{3,2,1,0:T(8,128)(2,1)S(1)} %collective-permute-done.2.before, ...), custom_call_target="tpu_custom_call" | custom-call | tf_op jit(solution)/shard_map/backward/pallas_call | solution.py:292
  82.2 4.4 %collective-permute-start.4 = (bf16[32,16,128]{2,1,0:T(8,128)(2,1)S(1)}, bf16[32,16,128]{2,1,0:T(8,128)(2,1)S(1)}, u32[]{:S(2)}, u32[]{:S(2)}) collective-permute-start(bf16[32,16,128]{2,1,0:T(8,128)(2,1)S(1)} %get-tuple-element.20.hi), channel_id=1, source_target_pairs={{0,1},{1,2},{2,3},{3,4},{4,5},{5,6},{6,7},{7,8},{8,9},{9,10},{10,1... | collective-permute-start | bytes 393224 | tf_op jit(solution)/shard_map/ppermute | solution.py:287
  86.6 1.9 %collective-permute-start.5 = (bf16[32,16,128]{2,1,0:T(8,128)(2,1)S(1)}, bf16[32,16,128]{2,1,0:T(8,128)(2,1)S(1)}, u32[]{:S(2)}, u32[]{:S(2)}) collective-permute-start(bf16[32,16,128]{2,1,0:T(8,128)(2,1)S(1)} %get-tuple-element.21.lo), channel_id=1, source_target_pairs={{1,0},{2,1},{3,2},{4,3},{5,4},{6,5},{7,6},{8,7},{9,8},{10,9},{11,1... | collective-permute-start | bytes 393224 | tf_op jit(solution)/shard_map/ppermute | solution.py:288
  88.5 1.4 %collective-permute-done.4.before = bf16[32,16,128]{2,1,0:T(8,128)(2,1)S(1)} collective-permute-done((bf16[32,16,128]{2,1,0:T(8,128)(2,1)S(1)}, bf16[32,16,128]{2,1,0:T(8,128)(2,1)S(1)}, u32[]{:S(2)}, u32[]{:S(2)}) %collective-permute-start.4) | collective-permute-done | bytes 131104 | tf_op jit(solution)/shard_map/ppermute | solution.py:287
  89.9 3.0 %collective-permute-done.5.after = bf16[32,16,128]{2,1,0:T(8,128)(2,1)S(1)} collective-permute-done((bf16[32,16,128]{2,1,0:T(8,128)(2,1)S(1)}, bf16[32,16,128]{2,1,0:T(8,128)(2,1)S(1)}, u32[]{:S(2)}, u32[]{:S(2)}) %collective-permute-start.5) | collective-permute-done | bytes 131104 | tf_op jit(solution)/shard_map/ppermute | solution.py:288
  92.9 6.9 %forward.3 = (bf16[8,32,16,128]{3,2,1,0:T(8,128)(2,1)S(1)}, bf16[8,32,16,128]{3,2,1,0:T(8,128)(2,1)S(1)}) custom-call(f32[8]{0:T(128)S(1)} %broadcast_divide_fusion.scales_ref, f32[8,2,3,128]{3,2,1,0:T(4,128)S(1)} %pad.7.taps_ref, f32[8,2,3,128]{3,2,1,0:T(4,128)S(1)} %pad.8.flip_ref, bf16[32,16,128]{2,1,0:T(8,128)(2,1)S(1)} %collective-permute-done.4.before, ...), custom_call_target="tpu_custom_call" | custom-call | tf_op jit(solution)/shard_map/forward/pallas_call | solution.py:289
  99.8 1.9 %collective-permute-start.6 = (bf16[8,32,16,128]{3,2,1,0:T(8,128)(2,1)S(1)}, bf16[8,32,16,128]{3,2,1,0:T(8,128)(2,1)S(1)}, u32[]{:S(2)}, u32[]{:S(2)}) collective-permute-start(bf16[8,32,16,128]{3,2,1,0:T(8,128)(2,1)S(1)} %get-tuple-element.22.hi), channel_id=1, source_target_pairs={{0,1},{1,2},{2,3},{3,4},{4,5},{5,6},{6,7},{7,8},{8,9},{9,10},{10,1... | collective-permute-start | bytes 3145736 | tf_op jit(solution)/shard_map/ppermute | solution.py:290
  101.7 2.5 %collective-permute-start.7 = (bf16[8,32,16,128]{3,2,1,0:T(8,128)(2,1)S(1)}, bf16[8,32,16,128]{3,2,1,0:T(8,128)(2,1)S(1)}, u32[]{:S(2)}, u32[]{:S(2)}) collective-permute-start(bf16[8,32,16,128]{3,2,1,0:T(8,128)(2,1)S(1)} %get-tuple-element.23.lo), channel_id=1, source_target_pairs={{1,0},{2,1},{3,2},{4,3},{5,4},{6,5},{7,6},{8,7},{9,8},{10,9},{11,1... | collective-permute-start | bytes 3145736 | tf_op jit(solution)/shard_map/ppermute | solution.py:291
  104.2 20.5 %collective-permute-done.6.before = bf16[8,32,16,128]{3,2,1,0:T(8,128)(2,1)S(1)} collective-permute-done((bf16[8,32,16,128]{3,2,1,0:T(8,128)(2,1)S(1)}, bf16[8,32,16,128]{3,2,1,0:T(8,128)(2,1)S(1)}, u32[]{:S(2)}, u32[]{:S(2)}) %collective-permute-start.6) | collective-permute-done | bytes 1048608 | tf_op jit(solution)/shard_map/ppermute | solution.py:290
  124.7 0.0 collective-permute-done.7.after
  124.7 6.9 %backward.3 = f32[1024,128]{1,0:T(8,128)} custom-call(f32[8,2,3,128]{3,2,1,0:T(4,128)S(1)} %pad.7.taps_ref, f32[8,2,3,128]{3,2,1,0:T(4,128)S(1)} %pad.8.flip_ref, bf16[8,32,16,128]{3,2,1,0:T(8,128)(2,1)S(1)} %collective-permute-done.6.before, bf16[8,32,16,128]{3,2,1,0:T(8,128)(2,1)S(1)} %get-tuple-element.23.lo, ...), custom_call_target="tpu_custom_call" | custom-call | tf_op jit(solution)/shard_map/backward/pallas_call | solution.py:292
  (4 shorter events, 0.0 us)
Async XLA Ops:
  0.0 34.0 %copy-start = (bf16[8,32,32,128]{3,2,1,0:T(8,128)(2,1)S(1)}, bf16[8,32,32,128]{3,2,1,0:T(8,128)(2,1)}, u32[]{:S(2)}) copy-start(bf16[8,32,32,128]{3,2,1,0:T(8,128)(2,1)} %raw_ref.5) | copy-start | bytes 6291460
  0.0 42.6 %copy-start.1 = (f32[8,2,3,31]{3,1,2,0:T(2,128)S(1)}, f32[8,2,3,31]{3,1,2,0:T(2,128)}, u32[]{:S(2)}) copy-start(f32[8,2,3,31]{3,1,2,0:T(2,128)} %param.3) | copy-start | bytes 17860
  35.0 7.8 %collective-permute-start = (bf16[32,16,128]{2,1,0:T(8,128)(2,1)S(1)}, bf16[32,16,128]{2,1,0:T(8,128)(2,1)S(1)}, u32[]{:S(2)}, u32[]{:S(2)}) collective-permute-start(bf16[32,16,128]{2,1,0:T(8,128)(2,1)S(1)} %get-tuple-element.15.hi), channel_id=1, source_target_pairs={{0,1},{1,2},{2,3},{3,4},{4,5},{5,6},{6,7},{7,8},{8,9},{9,10},{10,1... | collective-permute-start | bytes 393224 | tf_op jit(solution)/shard_map/ppermute | solution.py:287
  38.0 6.3 %collective-permute-start.1 = (bf16[32,16,128]{2,1,0:T(8,128)(2,1)S(1)}, bf16[32,16,128]{2,1,0:T(8,128)(2,1)S(1)}, u32[]{:S(2)}, u32[]{:S(2)}) collective-permute-start(bf16[32,16,128]{2,1,0:T(8,128)(2,1)S(1)} %get-tuple-element.16.lo), channel_id=1, source_target_pairs={{1,0},{2,1},{3,2},{4,3},{5,4},{6,5},{7,6},{8,7},{9,8},{10,9},{11,1... | collective-permute-start | bytes 393224 | tf_op jit(solution)/shard_map/ppermute | solution.py:288
  51.2 24.9 %collective-permute-start.2 = (bf16[8,32,16,128]{3,2,1,0:T(8,128)(2,1)S(1)}, bf16[8,32,16,128]{3,2,1,0:T(8,128)(2,1)S(1)}, u32[]{:S(2)}, u32[]{:S(2)}) collective-permute-start(bf16[8,32,16,128]{3,2,1,0:T(8,128)(2,1)S(1)} %get-tuple-element.17.hi), channel_id=1, source_target_pairs={{0,1},{1,2},{2,3},{3,4},{4,5},{5,6},{6,7},{7,8},{8,9},{9,10},{10,1... | collective-permute-start | bytes 3145736 | tf_op jit(solution)/shard_map/ppermute | solution.py:290
  53.1 23.0 %collective-permute-start.3 = (bf16[8,32,16,128]{3,2,1,0:T(8,128)(2,1)S(1)}, bf16[8,32,16,128]{3,2,1,0:T(8,128)(2,1)S(1)}, u32[]{:S(2)}, u32[]{:S(2)}) collective-permute-start(bf16[8,32,16,128]{3,2,1,0:T(8,128)(2,1)S(1)} %get-tuple-element.18.lo), channel_id=1, source_target_pairs={{1,0},{2,1},{3,2},{4,3},{5,4},{6,5},{7,6},{8,7},{9,8},{10,9},{11,1... | collective-permute-start | bytes 3145736 | tf_op jit(solution)/shard_map/ppermute | solution.py:291
  82.2 7.7 %collective-permute-start.4 = (bf16[32,16,128]{2,1,0:T(8,128)(2,1)S(1)}, bf16[32,16,128]{2,1,0:T(8,128)(2,1)S(1)}, u32[]{:S(2)}, u32[]{:S(2)}) collective-permute-start(bf16[32,16,128]{2,1,0:T(8,128)(2,1)S(1)} %get-tuple-element.20.hi), channel_id=1, source_target_pairs={{0,1},{1,2},{2,3},{3,4},{4,5},{5,6},{6,7},{7,8},{8,9},{9,10},{10,1... | collective-permute-start | bytes 393224 | tf_op jit(solution)/shard_map/ppermute | solution.py:287
  86.6 6.3 %collective-permute-start.5 = (bf16[32,16,128]{2,1,0:T(8,128)(2,1)S(1)}, bf16[32,16,128]{2,1,0:T(8,128)(2,1)S(1)}, u32[]{:S(2)}, u32[]{:S(2)}) collective-permute-start(bf16[32,16,128]{2,1,0:T(8,128)(2,1)S(1)} %get-tuple-element.21.lo), channel_id=1, source_target_pairs={{1,0},{2,1},{3,2},{4,3},{5,4},{6,5},{7,6},{8,7},{9,8},{10,9},{11,1... | collective-permute-start | bytes 393224 | tf_op jit(solution)/shard_map/ppermute | solution.py:288
  99.8 24.9 %collective-permute-start.6 = (bf16[8,32,16,128]{3,2,1,0:T(8,128)(2,1)S(1)}, bf16[8,32,16,128]{3,2,1,0:T(8,128)(2,1)S(1)}, u32[]{:S(2)}, u32[]{:S(2)}) collective-permute-start(bf16[8,32,16,128]{3,2,1,0:T(8,128)(2,1)S(1)} %get-tuple-element.22.hi), channel_id=1, source_target_pairs={{0,1},{1,2},{2,3},{3,4},{4,5},{5,6},{6,7},{7,8},{8,9},{9,10},{10,1... | collective-permute-start | bytes 3145736 | tf_op jit(solution)/shard_map/ppermute | solution.py:290
  101.7 23.0 %collective-permute-start.7 = (bf16[8,32,16,128]{3,2,1,0:T(8,128)(2,1)S(1)}, bf16[8,32,16,128]{3,2,1,0:T(8,128)(2,1)S(1)}, u32[]{:S(2)}, u32[]{:S(2)}) collective-permute-start(bf16[8,32,16,128]{3,2,1,0:T(8,128)(2,1)S(1)} %get-tuple-element.23.lo), channel_id=1, source_target_pairs={{1,0},{2,1},{3,2},{4,3},{5,4},{6,5},{7,6},{8,7},{9,8},{10,9},{11,1... | collective-permute-start | bytes 3145736 | tf_op jit(solution)/shard_map/ppermute | solution.py:291

commit v2 on v1

v2 whole, which is shorter than its diff:
```python
import functools

import jax
import jax.numpy as jnp
from jax import lax
from jax.experimental import pallas as pl
from jax.experimental.pallas import tpu as pltpu
from jax.sharding import PartitionSpec as P

ITERS = 2
LANES = 128
F32 = jnp.float32
BF16 = jnp.bfloat16


def toeplitz(row, rows, offset):
    lanes = row.shape[-1]
    wide = jnp.broadcast_to(row, (rows, lanes))
    return pltpu.roll(wide, (-offset) % lanes, 1, stride=1, stride_axis=0)


def depth_table(row, planes, radius, swapped):
    offset = radius - planes // 2
    lanes = row.shape[-1]
    ahead = pltpu.roll(row, lanes - planes, 1)
    behind = pltpu.roll(row, planes, 1)
    near = toeplitz(jnp.where(swapped == 1, ahead, row), planes, offset)
    far = toeplitz(jnp.where(swapped == 1, behind, row), planes, offset)
    lane = lax.broadcasted_iota(jnp.int32, near.shape, 1)
    return jnp.where(lane < planes, near, far).astype(BF16)[:, : 2 * planes]


def width_table(row, width, radius):
    table = toeplitz(row, width, radius)
    r = lax.broadcasted_iota(jnp.int32, table.shape, 0)
    l = lax.broadcasted_iota(jnp.int32, table.shape, 1)
    return jnp.where(jnp.abs(l - r) <= radius, table, 0.0)


def height_table(rows, height, radius):
    lane = lax.broadcasted_iota(jnp.int32, (height, rows[0].shape[-1]), 1)
    table = jnp.zeros(lane.shape, F32)
    for t, row in enumerate(rows):
        part = toeplitz(row, height, radius - t * height)
        table = jnp.where(lane // height == t, part, table)
    return table[:, : len(rows) * height].astype(BF16)


def store_width_table(bx_ref, rows, width, radius):
    for t, row in enumerate(rows):
        for s in range(len(rows)):
            block = (
                width_table(row, width, radius)
                if s == t
                else jnp.zeros((width, width), F32)
            )
            bx_ref[pl.ds(t * width, width), pl.ds(s * width, width)] = block.astype(BF16)


def depth_pass(parts, bz, zs_ref):
    height, _, width = parts[0].shape
    for y in range(0, height, 2):
        rhs = jnp.concatenate(
            [jnp.concatenate([p[yy] for p in parts], axis=0) for yy in (y, y + 1)], axis=1
        )
        out = jnp.dot(bz, rhs, preferred_element_type=F32).astype(BF16)
        zs_ref[y] = out[:, :width]
        zs_ref[y + 1] = out[:, width:]


def width_pass(zs_at, bx, xs_ref, height, planes, terms, width, group):
    for g in range(0, height, group):
        lhs = jnp.concatenate(
            [
                jnp.concatenate([zs_at(y, t) for t in range(terms)], axis=1)
                for y in range(g, g + group)
            ],
            axis=0,
        )
        out = jnp.dot(lhs, bx, preferred_element_type=F32)
        for t in range(terms):
            for i in range(group):
                xs_ref[t, pl.ds((g + i) * (planes + 1), planes), :] = out[
                    i * planes : (i + 1) * planes, t * width : (t + 1) * width
                ]


def height_pair(xs_ref, by, z, height, planes, terms, width):
    rhs = jnp.concatenate(
        [
            jnp.concatenate(
                [
                    xs_ref[t, pl.ds(zz, height, stride=planes + 1), :].astype(BF16)
                    for t in range(terms)
                ],
                axis=0,
            )
            for zz in (z, z + 1)
        ],
        axis=1,
    )
    out = jnp.dot(by, rhs, preferred_element_type=F32)
    return out[:, :width], out[:, width:]


def swap_out(qs_ref, put, height, planes):
    for y in range(height):
        put(y, qs_ref[pl.ds(y, planes, stride=height + 1), :].astype(BF16))


def sums_body(even_ref, raw_ref, sums_ref, near_ref, far_ref):
    views, planes, height, width = raw_ref.shape
    half = planes // 2
    even = even_ref[0]
    for v in range(views):
        acc = jnp.zeros((height, width), F32)
        for z in range(planes):
            acc = acc + raw_ref[v, z].astype(F32)
        row = jnp.sum(acc, axis=0, keepdims=True)
        sums_ref[pl.ds(v, 1), :] = jnp.broadcast_to(
            jnp.sum(row, axis=1, keepdims=True), (1, width)
        )
        near_ref[v] = raw_ref[v, pl.ds(even * half, half)]
        far_ref[v] = raw_ref[v, pl.ds((1 - even) * half, half)]


def scale_rows(totals_ref):
    totals = totals_ref[...]
    return jnp.mean(totals, axis=0, keepdims=True) / totals


def first_body(totals_ref, raw_ref, est_ref, slab_ref, qs_ref):
    views, planes, height, width = raw_ref.shape
    scales = scale_rows(totals_ref)
    for z in range(planes):
        acc = scales[0:1] * raw_ref[0, z].astype(F32)
        for v in range(1, views):
            acc = acc + scales[v : v + 1] * raw_ref[v, z].astype(F32)
        acc = acc / views
        est_ref[pl.ds(z * height, height), :] = acc
        qs_ref[pl.ds(z * (height + 1), height), :] = acc

    def put(y, value):
        slab_ref[y] = value

    swap_out(qs_ref, put, height, planes)


def forward_body(radius, swapped_ref, pad_ref, totals_ref, taps_ref, flip_ref, own_ref, part_ref,
                 raw_ref, raw_part_ref, q_ref, bz_ref, bx_ref, zs_ref, xs_ref, qs_ref, sc_ref):
    views, planes, height, width = raw_ref.shape
    terms = taps_ref.shape[1]
    half = planes // 2
    swapped = swapped_ref[0]
    pad = pad_ref[0]
    sc_ref[...] = scale_rows(totals_ref)
    for v in range(views):
        for t in range(terms):
            bz_ref[pl.ds((v * terms + t) * planes, planes), :] = depth_table(
                taps_ref[v, t, 0:1, :], planes, radius, swapped
            )
    depth_pass((own_ref, part_ref), bz_ref[...], zs_ref)

    def view(v, carry):
        store_width_table(bx_ref, [flip_ref[v, t, 2:3, :] for t in range(terms)], width, radius)
        by = height_table([taps_ref[v, t, 1:2, :] for t in range(terms)], height, radius)
        scale = sc_ref[pl.ds(v, 1), :]

        def zs_at(y, t):
            start = pl.multiple_of((v * terms + t) * planes, planes)
            return zs_ref[y, pl.ds(start, planes), :]

        width_pass(zs_at, bx_ref[...], xs_ref, height, planes, terms, width, 8)
        for partner in (False, True):
            base = (1 - swapped if partner else swapped) * half
            for r in range(0, half, 2):
                pair = height_pair(xs_ref, by, base + r, height, planes, terms, width)
                for i, blurred in enumerate(pair):
                    if partner:
                        raw = raw_part_ref[v, r + i]
                        blurred = blurred + pad
                    else:
                        raw = raw_ref[v, (1 - swapped) * half + r + i]
                    rows = pl.ds((base + r + i) * (height + 1), height)
                    qs_ref[rows, :] = scale * raw.astype(F32) / blurred

        def put(y, value):
            q_ref[v, y] = value

        swap_out(qs_ref, put, height, planes)
        return carry

    lax.fori_loop(0, views, view, 0)


def backward_body(radius, last, swapped_ref, taps_ref, flip_ref, near_ref, far_ref, est_ref, *refs):
    if last:
        new_ref, bx_ref, zs_ref, xs_ref, fac_ref, qs_ref = refs
    else:
        new_ref, slab_ref, bx_ref, zs_ref, xs_ref, fac_ref, qs_ref = refs
    views, height, planes, width = near_ref.shape
    terms = taps_ref.shape[1]
    swapped = swapped_ref[0]
    fac_ref[...] = jnp.ones(fac_ref.shape, F32)

    def view(v, carry):
        bz = jnp.concatenate(
            [depth_table(flip_ref[v, t, 0:1, :], planes, radius, swapped) for t in range(terms)],
            axis=0,
        )
        store_width_table(bx_ref, [taps_ref[v, t, 2:3, :] for t in range(terms)], width, radius)
        by = height_table([flip_ref[v, t, 1:2, :] for t in range(terms)], height, radius)
        depth_pass((near_ref.at[v], far_ref.at[v]), bz, zs_ref)

        def zs_at(y, t):
            return zs_ref[y, t * planes : (t + 1) * planes, :]

        width_pass(zs_at, bx_ref[...], xs_ref, height, planes, terms, width, 8)
        for z in range(0, planes, 2):
            pair = height_pair(xs_ref, by, z, height, planes, terms, width)
            for i, blurred in enumerate(pair):
                rows = pl.ds((z + i) * height, height)
                fac_ref[rows, :] = fac_ref[rows, :] * blurred
        return carry

    lax.fori_loop(0, views, view, 0)
    for z in range(planes):
        rows = pl.ds(z * height, height)
        new = est_ref[rows, :] * fac_ref[rows, :]
        new_ref[rows, :] = new
        if not last:
            qs_ref[pl.ds(z * (height + 1), height), :] = new
    if not last:

        def put(y, value):
            slab_ref[y] = value

        swap_out(qs_ref, put, height, planes)


VMEM_SPEC = pl.BlockSpec(memory_space=pltpu.VMEM)
SMEM_SPEC = pl.BlockSpec(memory_space=pltpu.SMEM)


def sum_over(value, axis, size):
    if size & (size - 1):
        return lax.psum(value, axis)
    step = 1
    while step < size:
        value = value + lax.ppermute(value, axis, [(i, i ^ step) for i in range(size)])
        step *= 2
    return value


def local(raw_views, spread_taps):
    views, planes, height, width = raw_views.shape
    terms, tap_count = spread_taps.shape[1], spread_taps.shape[3]
    radius = (tap_count - 1) // 2
    half = planes // 2
    cells = planes * height
    size = lax.axis_size("tile")
    place = lax.axis_index("tile")
    odd = lax.rem(place, 2)
    even = 1 - odd
    near_pairs = [(i, i + 1) for i in range(0, size - 1, 2)]
    far_pairs = [(i, i + 1) for i in range(1, size - 1, 2)]
    near_pairs += [(j, i) for i, j in near_pairs]
    far_pairs += [(j, i) for i, j in far_pairs]
    near_at = place + even - odd
    far_at = place + odd - even

    def missing(at):
        return jnp.where((at < 0) | (at >= size), 1.0, 0.0).astype(F32).reshape(1)

    near_pad, far_pad = missing(near_at), missing(far_at)
    even, odd = even.reshape(1), odd.reshape(1)

    taps = spread_taps.astype(BF16).astype(F32)
    lane_pad = ((0, 0), (0, 0), (0, 0), (0, LANES - tap_count))
    flip = jnp.pad(taps[:, :, :, ::-1], lane_pad)
    taps = jnp.pad(taps, lane_pad)

    flat = jax.ShapeDtypeStruct((cells, width), F32)
    slab = jax.ShapeDtypeStruct((height, planes, width), BF16)
    halves = jax.ShapeDtypeStruct((views, half, height, width), BF16)
    windows = jax.ShapeDtypeStruct((views, height, planes, width), BF16)
    params = pltpu.CompilerParams(vmem_limit_bytes=24 * 1024 * 1024)
    turned = pltpu.VMEM((planes * (height + 1), width), F32)
    spread = pltpu.VMEM((terms, height * (planes + 1), width), F32)
    square = pltpu.VMEM((terms * width, terms * width), BF16)

    sums, raw_near, raw_far = pl.pallas_call(
        sums_body,
        out_shape=(jax.ShapeDtypeStruct((views, width), F32), halves, halves),
        in_specs=[SMEM_SPEC, VMEM_SPEC],
        out_specs=(VMEM_SPEC,) * 3,
        compiler_params=params,
        name="sums",
    )(even, raw_views)
    raw_far = lax.ppermute(raw_far, "tile", far_pairs)
    raw_near = lax.ppermute(raw_near, "tile", near_pairs)
    totals = sum_over(sums, "tile", size)

    estimate, own = pl.pallas_call(
        first_body,
        out_shape=(flat, slab),
        in_specs=[VMEM_SPEC, VMEM_SPEC],
        out_specs=(VMEM_SPEC,) * 2,
        scratch_shapes=[turned],
        compiler_params=params,
        name="first",
    )(totals, raw_views)

    forward = pl.pallas_call(
        functools.partial(forward_body, radius),
        out_shape=windows,
        in_specs=[SMEM_SPEC] * 2 + [VMEM_SPEC] * 7,
        out_specs=VMEM_SPEC,
        scratch_shapes=[
            pltpu.VMEM((views * terms * planes, 2 * planes), BF16),
            square,
            pltpu.VMEM((height, views * terms * planes, width), BF16),
            spread,
            turned,
            pltpu.VMEM((views, width), F32),
        ],
        compiler_params=params,
        name="forward",
    )

    def backward(last):
        return pl.pallas_call(
            functools.partial(backward_body, radius, last),
            out_shape=(flat,) if last else (flat, slab),
            in_specs=[SMEM_SPEC] + [VMEM_SPEC] * 5,
            out_specs=(VMEM_SPEC,) * (1 if last else 2),
            scratch_shapes=[
                square,
                pltpu.VMEM((height, terms * planes, width), BF16),
                spread,
                pltpu.VMEM((cells, width), F32),
                turned,
            ],
            compiler_params=params,
            name="backward",
        )

    for iteration in range(ITERS):
        last = iteration == ITERS - 1
        far = lax.ppermute(own, "tile", far_pairs)
        near = lax.ppermute(own, "tile", near_pairs)
        q_near = forward(odd, near_pad, totals, taps, flip, own, near, raw_views, raw_near)
        q_far = forward(even, far_pad, totals, taps, flip, own, far, raw_views, raw_far)
        out = backward(last)(even, taps, flip, q_near, q_far, estimate)
        if last:
            (estimate,) = out
        else:
            estimate, own = out
    return estimate.reshape(planes, height, width)


def solution(mesh):
    return jax.shard_map(
        local,
        mesh=mesh,
        in_specs=(P(None, ("blocks", "tile"), None, None), P()),
        out_specs=P(("blocks", "tile"), None, None),
        check_vma=False,
    )
```

time: 132 us -> 98.3 us (0.74)
  blocking collectives: 30.5 us -> 0 us
  Pallas kernels: 27.8 us -> 46.7 us
  waiting for transfers between devices: 46.8 us -> 29.4 us
  starting transfers between devices: 22.7 us -> 19.2 us
  other arithmetic: 2.82 us -> 0.02 us
  local copies, waits for them, and re-layouts: 0.14 us -> 2.52 us
    psum x1 -> x0, blocking collectives: 30.5 us -> none  [local(): totals = lax.psum(jnp.sum(raw_views, axis=(1, 2, 3), dtype=F32), 'tile')]
    pallas_call x5 -> x8, Pallas kernels: 27.8 us -> 46.7 us  [the longest x2 16 us: local(): forward(odd, near_pad, totals, taps, flip, own, near, raw_views, raw_near)]
    ppermute x8 -> x10, waiting for transfers between devices: 46.8 us -> 29.4 us  [the longest x4 23.7 us: sum_over(): lax.ppermute(value, axis, [(i, i ^ step) for i in range(size)])]
    ppermute x8 -> x10, starting transfers between devices: 22.7 us -> 19.2 us  [the longest x2 8.94 us: local(): far = lax.ppermute(own, 'tile', far_pairs)]
    reduce_sum x2 -> x0, other arithmetic: 2.81 us -> none  [the longest x1 2.2 us: local(): totals = lax.psum(jnp.sum(raw_views, axis=(1, 2, 3), dtype=F32), 'tile')]
    unnamed x4 -> x10, local copies, waits for them, and re-layouts: 0.01 us -> 2.39 us
  transfers between devices with their start and end apart: 8 -> 10, of which waited for: 5 -> 5; matrix products, arithmetic and copies ran while one was open for 0% -> 0% of each run, Pallas kernels for 0% -> 16%
where the time goes in v2:
time: 98.3 us; the launch traced here: 98 us
  Pallas kernels  46.7 us (48%)
  waiting for transfers between devices  29.4 us (30%)
  starting transfers between devices  19.2 us (20%)
  local copies, waits for them, and re-layouts  2.52 us (3%)
    ppermute x4, waiting for transfers between devices, sum_over(): lax.ppermute(value, axis, [(i, i ^ step) for i in range(size)])  23.7 us
    pallas_call x2, Pallas kernels, local(): forward(odd, near_pad, totals, taps, flip, own, near, raw_views, raw_near)  16 us
    pallas_call x2, Pallas kernels, local(): forward(even, far_pad, totals, taps, flip, own, far, raw_views, raw_far)  14.4 us
    pallas_call x2, Pallas kernels, local(): out = backward(last)(even, taps, flip, q_near, q_far, estimate)  14.2 us
    ppermute x2, starting transfers between devices, local(): far = lax.ppermute(own, 'tile', far_pairs)  8.94 us
    ppermute x2, waiting for transfers between devices, local(): far = lax.ppermute(own, 'tile', far_pairs)  5.69 us
    ppermute x4, starting transfers between devices, sum_over(): lax.ppermute(value, axis, [(i, i ^ step) for i in range(size)])  5.37 us
    ppermute x1, starting transfers between devices, local(): raw_far = lax.ppermute(raw_far, 'tile', far_pairs)  4.49 us
  transfers between devices with their start and end apart: 10, of which 5 were waited for; matrix products, arithmetic and copies ran while one was open for 0% of the time, Pallas kernels for 16%

profile of v2, /device:TPU:1, one launch (start us, length us, event | category | flops | bytes accessed | tf_op | source)
XLA Modules:
  0.0 98.0 jit_solution(12523131054394507448)
XLA Ops:
  0.0 1.6 %copy-done = bf16[8,32,32,128]{3,2,1,0:T(8,128)(2,1)S(1)} copy-done((bf16[8,32,32,128]{3,2,1,0:T(8,128)(2,1)S(1)}, bf16[8,32,32,128]{3,2,1,0:T(8,128)(2,1)}, u32[]{:S(2)}) %copy-start) | copy-done | bytes 2097176
  1.6 1.7 %sums.1 = (f32[8,128]{1,0:T(8,128)S(1)}, bf16[8,16,32,128]{3,2,1,0:T(8,128)(2,1)}, bf16[8,16,32,128]{3,2,1,0:T(8,128)(2,1)}) custom-call(s32[1]{0:T(128)} %bitcast.even_ref.swapped_ref, bf16[8,32,32,128]{3,2,1,0:T(8,128)(2,1)S(1)} %copy-done), custom_call_target="tpu_custom_call" | custom-call | tf_op jit(solution)/shard_map/sums/pallas_call | solution.py:292
  3.3 4.5 %collective-permute-start.7 = (bf16[8,16,32,128]{3,2,1,0:T(8,128)(2,1)}, bf16[8,16,32,128]{3,2,1,0:T(8,128)(2,1)S(1)}, u32[]{:S(2)}, u32[]{:S(2)}) collective-permute-start(bf16[8,16,32,128]{3,2,1,0:T(8,128)(2,1)} %get-tuple-element.15), channel_id=1, source_target_pairs={{1,2},{3,4},{5,6},{7,8},{9,10},{11,12},{13,14},{2,1},{4,3},{6,5},{... | collective-permute-start | bytes 3145736 | tf_op jit(solution)/shard_map/ppermute | solution.py:300
  7.8 0.1 collective-permute-start.5
  7.9 0.5 collective-permute-start
  8.4 2.5 %collective-permute-done = f32[8,128]{1,0:T(8,128)S(1)} collective-permute-done((f32[8,128]{1,0:T(8,128)S(1)}, f32[8,128]{1,0:T(8,128)S(1)}, u32[]{:S(2)}, u32[]{:S(2)}) %collective-permute-start) | collective-permute-done | bytes 4128 | tf_op jit(solution)/shard_map/ppermute | solution.py:250
  10.9 1.3 %collective-permute-start.1 = (f32[8,128]{1,0:T(8,128)S(1)}, f32[8,128]{1,0:T(8,128)S(1)}, u32[]{:S(2)}, u32[]{:S(2)}) collective-permute-start(f32[8,128]{1,0:T(8,128)S(1)} %add.23), channel_id=1, source_target_pairs={{0,2},{1,3},{2,0},{3,1},{4,6},{5,7},{6,4},{7,5},{8,10},{9,11},{10,... | collective-permute-start | bytes 12296 | tf_op jit(solution)/shard_map/ppermute | solution.py:250
  12.1 19.0 %collective-permute-done.1 = f32[8,128]{1,0:T(8,128)S(1)} collective-permute-done((f32[8,128]{1,0:T(8,128)S(1)}, f32[8,128]{1,0:T(8,128)S(1)}, u32[]{:S(2)}, u32[]{:S(2)}) %collective-permute-start.1) | collective-permute-done | bytes 4128 | tf_op jit(solution)/shard_map/ppermute | solution.py:250
  31.1 1.3 %collective-permute-start.2 = (f32[8,128]{1,0:T(8,128)S(1)}, f32[8,128]{1,0:T(8,128)S(1)}, u32[]{:S(2)}, u32[]{:S(2)}) collective-permute-start(f32[8,128]{1,0:T(8,128)S(1)} %add.24), channel_id=1, source_target_pairs={{0,4},{1,5},{2,6},{3,7},{4,0},{5,1},{6,2},{7,3},{8,12},{9,13},{10,... | collective-permute-start | bytes 12296 | tf_op jit(solution)/shard_map/ppermute | solution.py:250
  32.4 1.2 %collective-permute-done.2 = f32[8,128]{1,0:T(8,128)S(1)} collective-permute-done((f32[8,128]{1,0:T(8,128)S(1)}, f32[8,128]{1,0:T(8,128)S(1)}, u32[]{:S(2)}, u32[]{:S(2)}) %collective-permute-start.2) | collective-permute-done | bytes 4128 | tf_op jit(solution)/shard_map/ppermute | solution.py:250
  33.6 2.3 %collective-permute-start.3 = (f32[8,128]{1,0:T(8,128)S(1)}, f32[8,128]{1,0:T(8,128)S(1)}, u32[]{:S(2)}, u32[]{:S(2)}) collective-permute-start(f32[8,128]{1,0:T(8,128)S(1)} %add.25), channel_id=1, source_target_pairs={{0,8},{1,9},{2,10},{3,11},{4,12},{5,13},{6,14},{7,15},{8,0},{9,1},... | collective-permute-start | bytes 12296 | tf_op jit(solution)/shard_map/ppermute | solution.py:250
  35.9 1.0 %collective-permute-done.3 = f32[8,128]{1,0:T(8,128)S(1)} collective-permute-done((f32[8,128]{1,0:T(8,128)S(1)}, f32[8,128]{1,0:T(8,128)S(1)}, u32[]{:S(2)}, u32[]{:S(2)}) %collective-permute-start.3) | collective-permute-done | bytes 4128 | tf_op jit(solution)/shard_map/ppermute | solution.py:250
  37.0 0.4 first.1
  37.4 0.0 copy-start.2
  37.4 0.8 copy-done.2
  38.2 4.4 %collective-permute-start.6 = (bf16[32,32,128]{2,1,0:T(8,128)(2,1)S(1)}, bf16[32,32,128]{2,1,0:T(8,128)(2,1)}, u32[]{:S(2)}, u32[]{:S(2)}) collective-permute-start(bf16[32,32,128]{2,1,0:T(8,128)(2,1)S(1)} %get-tuple-element.13.own_ref), channel_id=1, source_target_pairs={{1,2},{3,4},{5,6},{7,8},{9,10},{11,12},{13,14},{2,1},{4,3},{6,5},{... | collective-permute-start | bytes 786440 | tf_op jit(solution)/shard_map/ppermute | solution.py:350
  42.6 0.2 collective-permute-start.4
  42.9 0.1 rev.3
  43.1 5.7 %collective-permute-done.6.part_ref = bf16[32,32,128]{2,1,0:T(8,128)(2,1)} collective-permute-done((bf16[32,32,128]{2,1,0:T(8,128)(2,1)S(1)}, bf16[32,32,128]{2,1,0:T(8,128)(2,1)}, u32[]{:S(2)}, u32[]{:S(2)}) %collective-permute-start.6) | collective-permute-done | bytes 262176 | tf_op jit(solution)/shard_map/ppermute | solution.py:350
  48.8 0.0 collective-permute-done.7.raw_part_ref
  48.8 7.7 %forward.5.far_ref = bf16[8,32,32,128]{3,2,1,0:T(8,128)(2,1)S(1)} custom-call(s32[1]{0:T(128)} %bitcast.even_ref.swapped_ref, f32[1]{0:T(128)} %bitcast.3.pad_ref, f32[8,128]{1,0:T(8,128)S(1)} %add.26.totals_ref, f32[8,2,3,128]{3,2,1,0:T(4,128)S(1)} %pad.7.taps_ref, f32[8,2,3,128]{3,2,1,0:T(4,128)S(1)} %pad.8.flip_ref, ...), custom_call_target="tpu_custom_call" | custom-call | tf_op jit(solution)/shard_map/forward/pallas_call | solution.py:353
  56.4 0.0 collective-permute-done.4.part_ref
  56.4 0.0 collective-permute-done.5.raw_part_ref
  56.4 0.0 copy-start.3
  56.4 8.1 %forward.4.near_ref = bf16[8,32,32,128]{3,2,1,0:T(8,128)(2,1)S(1)} custom-call(s32[1]{0:T(128)} %bitcast.1.swapped_ref, f32[1]{0:T(128)} %bitcast.2.pad_ref, f32[8,128]{1,0:T(8,128)S(1)} %add.26.totals_ref, f32[8,2,3,128]{3,2,1,0:T(4,128)S(1)} %pad.7.taps_ref, f32[8,2,3,128]{3,2,1,0:T(4,128)S(1)} %pad.8.flip_ref, ...), custom_call_target="tpu_custom_call" | custom-call | tf_op jit(solution)/shard_map/forward/pallas_call | solution.py:352
  64.5 6.7 %backward.2 = (f32[1024,128]{1,0:T(8,128)S(1)}, bf16[32,32,128]{2,1,0:T(8,128)(2,1)S(1)}) custom-call(s32[1]{0:T(128)} %bitcast.even_ref.swapped_ref, f32[8,2,3,128]{3,2,1,0:T(4,128)S(1)} %pad.7.taps_ref, f32[8,2,3,128]{3,2,1,0:T(4,128)S(1)} %pad.8.flip_ref, bf16[8,32,32,128]{3,2,1,0:T(8,128)(2,1)S(1)} %forward.4.near_ref, ...), custom_call_target="tpu_custom_call" | custom-call | tf_op jit(solution)/shard_map/backward/pallas_call | solution.py:354
  71.3 0.1 collective-permute-start.8
  71.4 4.5 %collective-permute-start.9 = (bf16[32,32,128]{2,1,0:T(8,128)(2,1)S(1)}, bf16[32,32,128]{2,1,0:T(8,128)(2,1)S(1)}, u32[]{:S(2)}, u32[]{:S(2)}) collective-permute-start(bf16[32,32,128]{2,1,0:T(8,128)(2,1)S(1)} %get-tuple-element.17.own_ref), channel_id=1, source_target_pairs={{1,2},{3,4},{5,6},{7,8},{9,10},{11,12},{13,14},{2,1},{4,3},{6,5},{... | collective-permute-start | bytes 786440 | tf_op jit(solution)/shard_map/ppermute | solution.py:350
  75.9 0.0 collective-permute-done.8.part_ref
  75.9 7.9 %forward.6.near_ref = bf16[8,32,32,128]{3,2,1,0:T(8,128)(2,1)S(1)} custom-call(s32[1]{0:T(128)} %bitcast.1.swapped_ref, f32[1]{0:T(128)} %bitcast.2.pad_ref, f32[8,128]{1,0:T(8,128)S(1)} %add.26.totals_ref, f32[8,2,3,128]{3,2,1,0:T(4,128)S(1)} %pad.7.taps_ref, f32[8,2,3,128]{3,2,1,0:T(4,128)S(1)} %pad.8.flip_ref, ...), custom_call_target="tpu_custom_call" | custom-call | tf_op jit(solution)/shard_map/forward/pallas_call | solution.py:352
  83.8 6.7 %forward.7.far_ref = bf16[8,32,32,128]{3,2,1,0:T(8,128)(2,1)S(1)} custom-call(s32[1]{0:T(128)} %bitcast.even_ref.swapped_ref, f32[1]{0:T(128)} %bitcast.3.pad_ref, f32[8,128]{1,0:T(8,128)S(1)} %add.26.totals_ref, f32[8,2,3,128]{3,2,1,0:T(4,128)S(1)} %pad.7.taps_ref, f32[8,2,3,128]{3,2,1,0:T(4,128)S(1)} %pad.8.flip_ref, ...), custom_call_target="tpu_custom_call" | custom-call | tf_op jit(solution)/shard_map/forward/pallas_call | solution.py:353
  90.6 7.5 %backward.3 = f32[1024,128]{1,0:T(8,128)} custom-call(s32[1]{0:T(128)} %bitcast.even_ref.swapped_ref, f32[8,2,3,128]{3,2,1,0:T(4,128)S(1)} %pad.7.taps_ref, f32[8,2,3,128]{3,2,1,0:T(4,128)S(1)} %pad.8.flip_ref, bf16[8,32,32,128]{3,2,1,0:T(8,128)(2,1)S(1)} %forward.6.near_ref, bf16[8,32,32,128]{3,2,1,0:T(8,128)(2,1)S(1)} %forward.7.far_ref, ...), custom_call_target="tpu_custom_call" | custom-call | tf_op jit(solution)/shard_map/backward/pallas_call | solution.py:354
  (14 shorter events, 0.1 us)
Async XLA Ops:
  0.0 1.6 %copy-start = (bf16[8,32,32,128]{3,2,1,0:T(8,128)(2,1)S(1)}, bf16[8,32,32,128]{3,2,1,0:T(8,128)(2,1)}, u32[]{:S(2)}) copy-start(bf16[8,32,32,128]{3,2,1,0:T(8,128)(2,1)} %raw_ref.11) | copy-start | bytes 6291460
  1.6 35.4 %copy-start.1 = (bf16[8,32,32,128]{3,2,1,0:T(8,128)(2,1)S(1)}, bf16[8,32,32,128]{3,2,1,0:T(8,128)(2,1)}, u32[]{:S(2)}) copy-start(bf16[8,32,32,128]{3,2,1,0:T(8,128)(2,1)} %raw_ref.11) | copy-start | bytes 6291460
  1.6 41.3 %copy-start.4 = (f32[8,2,3,31]{3,1,2,0:T(2,128)S(1)}, f32[8,2,3,31]{3,1,2,0:T(2,128)}, u32[]{:S(2)}) copy-start(f32[8,2,3,31]{3,1,2,0:T(2,128)} %param.3) | copy-start | bytes 17860
  3.3 45.4 %collective-permute-start.7 = (bf16[8,16,32,128]{3,2,1,0:T(8,128)(2,1)}, bf16[8,16,32,128]{3,2,1,0:T(8,128)(2,1)S(1)}, u32[]{:S(2)}, u32[]{:S(2)}) collective-permute-start(bf16[8,16,32,128]{3,2,1,0:T(8,128)(2,1)} %get-tuple-element.15), channel_id=1, source_target_pairs={{1,2},{3,4},{5,6},{7,8},{9,10},{11,12},{13,14},{2,1},{4,3},{6,5},{... | collective-permute-start | bytes 3145736 | tf_op jit(solution)/shard_map/ppermute | solution.py:300
  7.8 48.6 %collective-permute-start.5 = (bf16[8,16,32,128]{3,2,1,0:T(8,128)(2,1)}, bf16[8,16,32,128]{3,2,1,0:T(8,128)(2,1)}, u32[]{:S(2)}, u32[]{:S(2)}) collective-permute-start(bf16[8,16,32,128]{3,2,1,0:T(8,128)(2,1)} %get-tuple-element.14), channel_id=1, source_target_pairs={{0,1},{2,3},{4,5},{6,7},{8,9},{10,11},{12,13},{14,15},{1,0},{3,2},... | collective-permute-start | bytes 3145736 | tf_op jit(solution)/shard_map/ppermute | solution.py:301
  7.9 3.0 %collective-permute-start = (f32[8,128]{1,0:T(8,128)S(1)}, f32[8,128]{1,0:T(8,128)S(1)}, u32[]{:S(2)}, u32[]{:S(2)}) collective-permute-start(f32[8,128]{1,0:T(8,128)S(1)} %get-tuple-element.12), channel_id=1, source_target_pairs={{0,1},{1,0},{2,3},{3,2},{4,5},{5,4},{6,7},{7,6},{8,9},{9,8},{10,11... | collective-permute-start | bytes 12296 | tf_op jit(solution)/shard_map/ppermute | solution.py:250
  10.9 20.2 %collective-permute-start.1 = (f32[8,128]{1,0:T(8,128)S(1)}, f32[8,128]{1,0:T(8,128)S(1)}, u32[]{:S(2)}, u32[]{:S(2)}) collective-permute-start(f32[8,128]{1,0:T(8,128)S(1)} %add.23), channel_id=1, source_target_pairs={{0,2},{1,3},{2,0},{3,1},{4,6},{5,7},{6,4},{7,5},{8,10},{9,11},{10,... | collective-permute-start | bytes 12296 | tf_op jit(solution)/shard_map/ppermute | solution.py:250
  31.1 2.5 %collective-permute-start.2 = (f32[8,128]{1,0:T(8,128)S(1)}, f32[8,128]{1,0:T(8,128)S(1)}, u32[]{:S(2)}, u32[]{:S(2)}) collective-permute-start(f32[8,128]{1,0:T(8,128)S(1)} %add.24), channel_id=1, source_target_pairs={{0,4},{1,5},{2,6},{3,7},{4,0},{5,1},{6,2},{7,3},{8,12},{9,13},{10,... | collective-permute-start | bytes 12296 | tf_op jit(solution)/shard_map/ppermute | solution.py:250
  33.6 3.4 %collective-permute-start.3 = (f32[8,128]{1,0:T(8,128)S(1)}, f32[8,128]{1,0:T(8,128)S(1)}, u32[]{:S(2)}, u32[]{:S(2)}) collective-permute-start(f32[8,128]{1,0:T(8,128)S(1)} %add.25), channel_id=1, source_target_pairs={{0,8},{1,9},{2,10},{3,11},{4,12},{5,13},{6,14},{7,15},{8,0},{9,1},... | collective-permute-start | bytes 12296 | tf_op jit(solution)/shard_map/ppermute | solution.py:250
  37.4 0.8 copy-start.2
  38.2 10.6 %collective-permute-start.6 = (bf16[32,32,128]{2,1,0:T(8,128)(2,1)S(1)}, bf16[32,32,128]{2,1,0:T(8,128)(2,1)}, u32[]{:S(2)}, u32[]{:S(2)}) collective-permute-start(bf16[32,32,128]{2,1,0:T(8,128)(2,1)S(1)} %get-tuple-element.13.own_ref), channel_id=1, source_target_pairs={{1,2},{3,4},{5,6},{7,8},{9,10},{11,12},{13,14},{2,1},{4,3},{6,5},{... | collective-permute-start | bytes 786440 | tf_op jit(solution)/shard_map/ppermute | solution.py:350
  42.6 13.8 %collective-permute-start.4 = (bf16[32,32,128]{2,1,0:T(8,128)(2,1)S(1)}, bf16[32,32,128]{2,1,0:T(8,128)(2,1)}, u32[]{:S(2)}, u32[]{:S(2)}) collective-permute-start(bf16[32,32,128]{2,1,0:T(8,128)(2,1)S(1)} %get-tuple-element.13.own_ref), channel_id=1, source_target_pairs={{0,1},{2,3},{4,5},{6,7},{8,9},{10,11},{12,13},{14,15},{1,0},{3,2},... | collective-permute-start | bytes 786440 | tf_op jit(solution)/shard_map/ppermute | solution.py:351
  56.4 8.1 %copy-start.3 = (f32[1024,128]{1,0:T(8,128)S(1)}, f32[1024,128]{1,0:T(8,128)}, u32[]{:S(2)}) copy-start(f32[1024,128]{1,0:T(8,128)} %copy-done.2) | copy-start | bytes 1572868
  71.3 4.6 %collective-permute-start.8 = (bf16[32,32,128]{2,1,0:T(8,128)(2,1)S(1)}, bf16[32,32,128]{2,1,0:T(8,128)(2,1)S(1)}, u32[]{:S(2)}, u32[]{:S(2)}) collective-permute-start(bf16[32,32,128]{2,1,0:T(8,128)(2,1)S(1)} %get-tuple-element.17.own_ref), channel_id=1, source_target_pairs={{0,1},{2,3},{4,5},{6,7},{8,9},{10,11},{12,13},{14,15},{1,0},{3,2},... | collective-permute-start | bytes 786440 | tf_op jit(solution)/shard_map/ppermute | solution.py:351
  71.4 12.5 %collective-permute-start.9 = (bf16[32,32,128]{2,1,0:T(8,128)(2,1)S(1)}, bf16[32,32,128]{2,1,0:T(8,128)(2,1)S(1)}, u32[]{:S(2)}, u32[]{:S(2)}) collective-permute-start(bf16[32,32,128]{2,1,0:T(8,128)(2,1)S(1)} %get-tuple-element.17.own_ref), channel_id=1, source_target_pairs={{1,2},{3,4},{5,6},{7,8},{9,10},{11,12},{13,14},{2,1},{4,3},{6,5},{... | collective-permute-start | bytes 786440 | tf_op jit(solution)/shard_map/ppermute | solution.py:350
